TPU v7x, 32 devices: a whole 2x2x4 slice. The times are simulated.
32 devices in a mesh: dom: 32 (over z, y, x, core).
Axes of the slice: x: 2, y: 2, z: 4, core: 2. Of those that a mesh axis runs over, the one named last changes fastest.
Arguments:
- features: bfloat16 [16384, 512], P('dom'), may hold values from -6 to 6
- weight: bfloat16 [512, 512], replicated, may hold values from -0.25 to 0.25
- grad_out: bfloat16 [16384, 512], P('dom'), may hold values from -6 to 6
- adjacency: bfloat16 [768, 128, 128], P('dom'), may hold values from -0.25 to 0.25
- tile_row: int32 [32, 24], P('dom'), may hold values from 0 to 3
- tile_src: int32 [32, 24], P('dom'), may hold values from 0 to 7
- tile_count: int32 [32], P('dom'), may hold values from 1 to 24, as said below
- send_tile: int32 [32, 4], P('dom'), may hold values from 0 to 3
- stale_feat: bfloat16 [32, 4, 128, 512], P('dom'), may hold values from -6 to 6
- stale_grad: bfloat16 [32, 4, 128, 512], P('dom'), may hold values from -6 to 6
- blend: float32 [512], replicated, may hold values from 0.2 to 0.8
Outputs:
- output: bfloat16 [16384, 512], P('dom')
- grad_features: bfloat16 [16384, 512], P('dom')
- grad_weight: bfloat16 [512, 512], replicated
Inputs may be any that keep to these rules, and one draw needn't show every extreme that they name: `tile_count`: counts are skewed; some partition holds all 24 entries.
All inputs are finite; a program needn't handle non-finite values.
Results may differ from a plain program's by a relative error of at most 0.0064.
Values may be sent and summed in bfloat16 or wider, within the bound.
A program may use at most 64 MiB of HBM per device.

v0:
```python
import functools

import jax
import jax.numpy as jnp
from jax import lax
from jax.experimental import pallas as pl
from jax.experimental.pallas import tpu as pltpu
from jax.sharding import PartitionSpec as P

MESH = pl.DeviceIdType.MESH
F32 = jnp.float32
BF16 = jnp.bfloat16


def bit_of(i, b):
    return lax.rem(lax.div(i, 1 << b), 2)


def flip(i, mask):
    out = i
    for b in range(mask.bit_length()):
        if mask >> b & 1:
            out = out + (1 - 2 * bit_of(i, b)) * (1 << b)
    return out


class Sems:
    def __init__(self, send, recv):
        self.send, self.recv, self.next = send, recv, 0

    def take(self):
        self.next += 1
        return self.next - 1


def names_and_shapes(tiles, block, width, entries, rounds, n_extra):
    nodes = tiles * block
    half, quarter, piece = width // 2, width // 8, width // 32
    v = pltpu.VMEM
    return dict(
        feat=v((tiles, block, width), BF16),
        wgt=v((width, width), BF16),
        gout=v((nodes, width), BF16),
        adj=v((entries, block, block), BF16),
        sfeat=v((rounds, block, width), BF16),
        sgrad=v((rounds, block, width), BF16),
        fsend=v((rounds, block, width), BF16),
        frecv=v((rounds, block, width), BF16),
        used=v((rounds, block, width), BF16),
        chain=v((entries + 1, block, block), F32),
        dense=v((nodes, (tiles + rounds) * block), BF16),
        part=v((nodes, width), F32),
        agg=v((nodes, width), BF16),
        outv=v((nodes, width), BF16),
        dpre=v((nodes, width), BF16),
        dagg=v((nodes, width), BF16),
        back=v((nodes, width), F32),
        gsend=v((rounds, block, width), BF16),
        grecv=v((rounds, block, width), BF16),
        gfeat=v((nodes, width), BF16),
        s0send=v((half, width), BF16),
        s0recv=v((half, width), BF16),
        acc=v((half, width), F32),
        s1send=v((half, width), BF16),
        s1recv=v((3, quarter, width), BF16),
        s2send=v((3, piece, width), BF16),
        s2recv=v((3, piece, width), BF16),
        xbuf=v((max(n_extra, 1), 4, piece, width), BF16),
        mine=v((piece, width), BF16),
        mixv=v((1, width), F32),
        row_s=pltpu.SMEM((1, entries), jnp.int32),
        src_s=pltpu.SMEM((1, entries), jnp.int32),
        tile_s=pltpu.SMEM((1, rounds), jnp.int32),
        lsem=pltpu.SemaphoreType.DMA((16,)),
        ssem=pltpu.SemaphoreType.DMA((96,)),
        rsem=pltpu.SemaphoreType.DMA((96,)),
    )


def kernel(names, nbits, *refs):
    (features, weight, grad_out, adjacency, stale_feat, stale_grad, blend,
     row_hbm, src_hbm, tile_hbm, tile_count, out_any, gf_any, gw_any) = refs[:14]
    s = dict(zip(names, refs[14:]))
    tile_row, tile_src, send_tile = s["row_s"], s["src_s"], s["tile_s"]
    tiles, block, width = s["feat"].shape
    rounds = s["fsend"].shape[0]
    entries = s["adj"].shape[0]
    nodes = tiles * block
    half, quarter, piece = width // 2, width // 8, width // 32
    me = lax.axis_index("dom")
    sems = Sems(s["ssem"], s["rsem"])
    pending = []

    def remote(src, dst, mask):
        i = sems.take()
        c = pltpu.make_async_remote_copy(
            src_ref=src, dst_ref=dst, send_sem=s["ssem"].at[i], recv_sem=s["rsem"].at[i],
            device_id=(flip(me, mask),), device_id_type=MESH)
        c.start()
        pending.append(c)
        return c

    loads = {}
    for i, (src, name) in enumerate((
            (tile_hbm, "tile_s"), (features, "feat"), (row_hbm, "row_s"), (src_hbm, "src_s"),
            (adjacency, "adj"), (blend, "mixv"), (stale_feat.at[0], "sfeat"),
            (weight, "wgt"), (grad_out, "gout"), (stale_grad.at[0], "sgrad"))):
        loads[name] = pltpu.make_async_copy(src, s[name], s["lsem"].at[i])
        loads[name].start()

    round_mask = [1 << (r * nbits // rounds) for r in range(rounds)]
    extra = []
    b = 5
    while b < nbits:
        extra.append((b, min(2, nbits - b)))
        b += 2
    peers = {1} | {k << 1 for k in (1, 2, 3)} | {k << 3 for k in (1, 2, 3)} | set(round_mask)
    for lo, nb in extra:
        peers |= {k << lo for k in range(1, 1 << nb)}
    barrier = pltpu.get_barrier_semaphore()
    for m in sorted(peers):
        pl.semaphore_signal(barrier, inc=1, device_id=(flip(me, m),), device_id_type=MESH)

    loads["tile_s"].wait()
    loads["feat"].wait()
    for r in range(rounds):
        s["fsend"][r] = s["feat"][send_tile[0, r]]
    pl.semaphore_wait(barrier, len(peers))
    fcopies = [remote(s["fsend"].at[r], s["frecv"].at[r], round_mask[r]) for r in range(rounds)]

    for name in ("row_s", "src_s"):
        loads[name].wait()
    live = tile_count[0]
    cells = tiles + rounds
    keys = [jnp.where(e < live, tile_row[0, e] * cells + tile_src[0, e], -1 - e) for e in range(entries)]
    loads["adj"].wait()
    s["chain"][0] = jnp.zeros((block, block), F32)
    for e in range(entries):
        prev = jnp.int32(0)
        for f in range(e):
            prev = jnp.where(keys[f] == keys[e], f + 1, prev)
        s["chain"][e + 1] = s["chain"][prev] + s["adj"][e].astype(F32)
    for t in range(tiles):
        for c in range(cells):
            last = jnp.int32(0)
            for e in range(entries):
                last = jnp.where(keys[e] == t * cells + c, e + 1, last)
            s["dense"][t * block:(t + 1) * block, c * block:(c + 1) * block] = s["chain"][last].astype(BF16)

    loads["mixv"].wait()
    mix = s["mixv"][...]
    keep = 1.0 - mix
    s["part"][...] = jnp.dot(s["dense"][:, :nodes], s["feat"][...].reshape(nodes, width),
                             preferred_element_type=F32)
    loads["sfeat"].wait()
    for r in range(rounds):
        fcopies[r].wait_recv()
        s["used"][r] = (keep * s["sfeat"][r].astype(F32) + mix * s["frecv"][r].astype(F32)).astype(BF16)
    loads["wgt"].wait()
    loads["gout"].wait()
    for t in range(tiles):
        rows = slice(t * block, (t + 1) * block)
        agg = (s["part"][rows, :] + jnp.dot(
            s["dense"][rows, nodes:], s["used"][...].reshape(rounds * block, width),
            preferred_element_type=F32)).astype(BF16)
        s["agg"][rows, :] = agg
        pre = jnp.dot(agg, s["wgt"][...], preferred_element_type=F32)
        sigma = jax.nn.sigmoid(pre)
        s["outv"][rows, :] = (pre * sigma).astype(BF16)
        s["dpre"][rows, :] = (s["gout"][rows, :].astype(F32) * sigma * (1.0 + pre * (1.0 - sigma))).astype(BF16)
    out_copy = pltpu.make_async_copy(s["outv"], out_any, s["lsem"].at[12])
    out_copy.start()

    j0 = bit_of(me, 0)
    j1 = lax.rem(lax.div(me, 2), 4)
    j2 = lax.rem(lax.div(me, 8), 4)

    def half_product(h):
        cols = pl.ds(pl.multiple_of(h * half, half), half)
        return lax.dot_general(s["agg"][:, cols], s["dpre"][...], (((0,), (0,)), ((), ())),
                               preferred_element_type=F32)

    def quarter_rows(k):
        return pl.ds(pl.multiple_of(flip(j1, k) * quarter, quarter), quarter)

    def piece_rows(k, base=0):
        return pl.ds(pl.multiple_of(base + flip(j2, k) * piece, piece), piece)

    s["s0send"][...] = half_product(1 - j0).astype(BF16)
    order1 = (3, 1, 2, 0)
    core = {}
    for k in order1:
        core[k] = remote(s["s0send"].at[quarter_rows(k)], s["s0recv"].at[quarter_rows(k)], 1)
    s["acc"][...] = half_product(j0)
    plane = {}
    for k in order1:
        core[k].wait_recv()
        total = s["acc"][quarter_rows(k), :] + s["s0recv"][quarter_rows(k), :].astype(F32)
        if k == 0:
            s["acc"][quarter_rows(0), :] = total
        else:
            s["s1send"][quarter_rows(k), :] = total.astype(BF16)
        if k == order1[2]:
            for kz in (3, 2, 1, 0):
                for kp in order1[:3]:
                    plane[kp, kz] = remote(s["s1send"].at[piece_rows(kz, flip(j1, kp) * quarter)],
                                           s["s1recv"].at[kp - 1, piece_rows(kz)], kp << 1)

    s["dagg"][...] = lax.dot_general(s["dpre"][...], s["wgt"][...], (((1,), (1,)), ((), ())),
                                     preferred_element_type=F32).astype(BF16)
    s["gsend"][...] = lax.dot_general(s["dense"][:, nodes:], s["dagg"][...], (((0,), (0,)), ((), ())),
                                      preferred_element_type=F32).astype(BF16).reshape(rounds, block, width)
    gcopies = {}
    late = [r for r in range(rounds) if round_mask[r] in (2, 4)]
    for r in [r for r in range(rounds) if r not in late] + late:
        gcopies[r] = remote(s["gsend"].at[r], s["grecv"].at[r], round_mask[r])
    s["back"][...] = lax.dot_general(s["dense"][:, :nodes], s["dagg"][...], (((0,), (0,)), ((), ())),
                                     preferred_element_type=F32)

    line = {}
    for kz in (3, 2, 1, 0):
        total = s["acc"][piece_rows(kz, j1 * quarter), :]
        for k in (1, 2, 3):
            plane[k, kz].wait_recv()
            total = total + s["s1recv"][k - 1, piece_rows(kz), :].astype(F32)
        if kz:
            s["s2send"][kz - 1] = total.astype(BF16)
            line[kz] = remote(s["s2send"].at[kz - 1], s["s2recv"].at[kz - 1], kz << 3)
    loads["sgrad"].wait()
    hot = [[jnp.where(send_tile[0, r] == t, 1.0, 0.0).astype(F32) for r in range(rounds)] for t in range(tiles)]

    def mix_rounds(which, dst):
        for r in which:
            gcopies[r].wait_recv()
        for t in range(tiles):
            rows = slice(t * block, (t + 1) * block)
            acc = s["back"][rows, :]
            for r in which:
                acc = acc + hot[t][r] * (keep * s["sgrad"][r].astype(F32) + mix * s["grecv"][r].astype(F32))
            s[dst][rows, :] = acc.astype(s[dst].dtype)

    mix_rounds([r for r in range(rounds) if r not in late], "back")
    for kz in (1, 2, 3):
        line[kz].wait_recv()
        total = total + s["s2recv"][kz - 1].astype(F32)
    for g, (lo, nb) in enumerate(extra):
        size = 1 << nb
        jx = lax.rem(lax.div(me, 1 << lo), size)
        s["xbuf"][g, pl.ds(jx, 1)] = total.astype(BF16)[None]
        swaps = [remote(s["xbuf"].at[g, jx], s["xbuf"].at[g, jx], k << lo) for k in range(1, size)]
        for c in swaps:
            c.wait_recv()
        total = s["xbuf"][g, 0].astype(F32)
        for x in range(1, size):
            total = total + s["xbuf"][g, x].astype(F32)

    def gw_rows(kc, kp, kz):
        at = flip(j0, kc) * half + flip(j1, kp) * quarter + flip(j2, kz) * piece
        return pl.ds(pl.multiple_of(at, piece), piece)

    arrivals = {}

    def forward(kc, kp, kz, level):
        dst = gw_any.at[gw_rows(kc, kp, kz)]
        ref = s["mine"] if level > 2 else dst
        if level > 2:
            for k in (3, 2, 1):
                arrivals[kc, kp, k] = remote(ref, dst, k << 3)
        if level > 1:
            for k in (3, 1, 2):
                arrivals[kc, k, kz] = remote(ref, dst, k << 1)
        arrivals[1, kp, kz] = remote(ref, dst, 1)

    s["mine"][...] = total.astype(BF16)
    forward(0, 0, 0, 3)
    own = pltpu.make_async_copy(s["mine"], gw_any.at[gw_rows(0, 0, 0)], s["lsem"].at[14])
    own.start()

    mix_rounds(late, "gfeat")
    gf_copy = pltpu.make_async_copy(s["gfeat"], gf_any, s["lsem"].at[13])
    gf_copy.start()

    for kz in (1, 2, 3):
        arrivals[0, 0, kz].wait_recv()
        forward(0, 0, kz, 2)
    for kz in (0, 1, 2, 3):
        for kp in (1, 2, 3):
            arrivals[0, kp, kz].wait_recv()
            forward(0, kp, kz, 1)
    for kz in range(4):
        for kp in range(4):
            arrivals[1, kp, kz].wait_recv()
    for c in pending:
        c.wait_send()
    own.wait()
    out_copy.wait()
    gf_copy.wait()


def finish(*refs):
    ins, outs, sem = refs[:3], refs[3:6], refs[6]
    parts = 1
    copies = []
    for i, (a, b) in enumerate(zip(ins, outs)):
        step = a.shape[0] // parts
        for q in range(parts):
            rows = pl.ds(q * step, step)
            copies.append(pltpu.make_async_copy(a.at[rows], b.at[rows], sem.at[i * parts + q]))
    for c in copies:
        c.start()
    for c in copies:
        c.wait()


def body(nbits, features, weight, grad_out, adjacency, tile_row, tile_src, tile_count,
         send_tile, stale_feat, stale_grad, blend):
    nodes, width = features.shape
    entries, block = adjacency.shape[:2]
    rounds = send_tile.shape[1]
    tiles = nodes // block
    n_extra = (max(nbits - 5, 0) + 1) // 2
    scratch = names_and_shapes(tiles, block, width, entries, rounds, n_extra)
    hbm = pl.BlockSpec(memory_space=pltpu.HBM)
    free = pl.BlockSpec(memory_space=pl.ANY)
    results = (jax.ShapeDtypeStruct((nodes, width), BF16),
               jax.ShapeDtypeStruct((nodes, width), BF16),
               jax.ShapeDtypeStruct((width, width), BF16))
    found = pl.pallas_call(
        functools.partial(kernel, tuple(scratch), nbits),
        name="layer",
        out_shape=results,
        in_specs=[hbm] * 10 + [pl.BlockSpec(memory_space=pltpu.SMEM)],
        out_specs=(free,) * 3,
        scratch_shapes=list(scratch.values()),
        compiler_params=pltpu.CompilerParams(collective_id=0, has_side_effects=True,
                                             vmem_limit_bytes=48 * 1024 * 1024),
    )(*(pltpu.with_memory_space_constraint(x, pltpu.HBM) for x in (
        features.reshape(tiles, block, width), weight, grad_out, adjacency, stale_feat, stale_grad,
        blend.reshape(1, width), tile_row, tile_src, send_tile)), tile_count)
    return tuple(pl.pallas_call(
        finish,
        name="finish",
        out_shape=results,
        in_specs=[free] * 3,
        out_specs=(hbm,) * 3,
        scratch_shapes=[pltpu.SemaphoreType.DMA((3,))],
        compiler_params=pltpu.CompilerParams(vmem_limit_bytes=16 * 1024 * 1024),
    )(*found))


def solution(mesh):
    nbits = mesh.shape["dom"].bit_length() - 1
    placed = (
        P("dom", None), P(), P("dom", None), P("dom", None, None), P("dom", None), P("dom", None),
        P("dom"), P("dom", None), P("dom", None, None, None), P("dom", None, None, None), P(),
    )
    return jax.shard_map(
        functools.partial(body, nbits),
        mesh=mesh,
        in_specs=placed,
        out_specs=(P("dom", None), P("dom", None), P()),
        check_vma=False,
    )
```

profile of v0, /device:TPU:0, one launch (start us, length us, event | category | flops | bytes accessed | tf_op | source)
XLA Modules:
  0.0 32.1 jit_solution(3688816447738086541)
XLA Ops:
  1.3 29.7 %layer.1 = (bf16[512,512]{1,0:T(8,128)(2,1)S(1)}, bf16[512,512]{1,0:T(8,128)(2,1)S(1)}, bf16[512,512]{1,0:T(8,128)(2,1)S(1)}) custom-call(bf16[4,128,512]{2,1,0:T(8,128)(2,1)} %bitcast.2, bf16[512,512]{1,0:T(8,128)(2,1)} %refs_1_.1, bf16[512,512]{1,0:T(8,128)(2,1)} %refs_2_.1, bf16[24,128,128]{2,1,0:T(8,128)(2,1)} %refs_3_.1, ...), custom_call_target="tpu_custom_call" | custom-call | tf_op jit(solution)/shard_map/layer/pallas_call | solution.py:328
  31.0 1.2 %finish.1 = (bf16[512,512]{1,0:T(8,128)(2,1)}, bf16[512,512]{1,0:T(8,128)(2,1)}, bf16[512,512]{1,0:T(8,128)(2,1)}) custom-call(bf16[512,512]{1,0:T(8,128)(2,1)S(1)} %get-tuple-element.6.refs_0_, bf16[512,512]{1,0:T(8,128)(2,1)S(1)} %get-tuple-element.7.refs_1_, bf16[512,512]{1,0:T(8,128)(2,1)S(1)} %get-tuple-element.8.refs_2_), custom_call_target="tpu_custom_call" | custom-call | tf_op jit(solution)/shard_map/finish/pallas_call | solution.py:340
where the time goes:
time: 32.3 us; the launch traced here: 32.1 us
  Pallas kernels  30.8 us (95%)
  between operations  1.29 us (4%)
    pallas_call x1, Pallas kernels, body(): pl.pallas_call(functools.partial(kernel, tuple(scratch), nbits), name='la...  29.7 us
    pallas_call x1, Pallas kernels, body(): pl.pallas_call(finish, name='finish', out_shape=results, in_specs=[free]...  1.17 us

commit v1 on v0

v1 whole, which is shorter than its diff:
```python
import functools

import jax
import jax.numpy as jnp
from jax import lax
from jax.experimental import pallas as pl
from jax.experimental.pallas import tpu as pltpu
from jax.sharding import PartitionSpec as P

MESH = pl.DeviceIdType.MESH
F32 = jnp.float32
BF16 = jnp.bfloat16
CHUNKS = 2
GROUP_BITS = 3
GROUP = 1 << GROUP_BITS
NEAR_LAST = (7, 6, 5, 3, 4, 2, 1)


def bit_of(i, b):
    return lax.rem(lax.div(i, 1 << b), 2)


class Index:
    def __init__(self, value, bits):
        self.value = value
        self.step = [(1 - 2 * bit_of(value, b)) * (1 << b) for b in range(bits)]

    def flip(self, mask):
        out = self.value
        for b in range(mask.bit_length()):
            if mask >> b & 1:
                out = out + self.step[b]
        return out


def upper_stages(nbits):
    stages, b = [], 1 + GROUP_BITS
    while b < nbits:
        stages.append((b, min(2, nbits - b)))
        b += 2
    return stages


def names_and_shapes(tiles, block, width, entries, rounds, n_upper):
    nodes = tiles * block
    half = width // 2
    piece = half // CHUNKS // GROUP
    v = pltpu.VMEM
    return dict(
        feat=v((tiles, block, width), BF16),
        wgt=v((width, width), BF16),
        gout=v((nodes, width), BF16),
        adj=v((entries, block, block), BF16),
        sfeat=v((rounds, block, width), BF16),
        sgrad=v((rounds * block, width), BF16),
        fsend=v((rounds, block, width), BF16),
        frecv=v((rounds, block, width), BF16),
        used=v((rounds * block, width), BF16),
        chain=v((entries + 1, block, block), F32),
        dense=v((nodes, (tiles + rounds) * block), BF16),
        pick=v((nodes, rounds * block), BF16),
        part=v((nodes, width), F32),
        aggt=v((width, nodes), BF16),
        outv=v((nodes, width), BF16),
        dpre=v((nodes, width), BF16),
        dagg=v((nodes, width), BF16),
        back=v((nodes, width), F32),
        gsend=v((rounds * block, width), BF16),
        grecv=v((rounds * block, width), BF16),
        gfeat=v((nodes, width), BF16),
        s0send=v((half, width), BF16),
        s0recv=v((half, width), BF16),
        acc=v((half, width), F32),
        s1send=v((half, width), BF16),
        s1recv=v((CHUNKS, (GROUP - 1) * piece, width), BF16),
        xbuf=v((max(n_upper, 1), CHUNKS, 4, piece, width), BF16),
        mine=v((CHUNKS, piece, width), BF16),
        mixv=v((1, width), F32),
        row_s=pltpu.SMEM((1, entries), jnp.int32),
        src_s=pltpu.SMEM((1, entries), jnp.int32),
        tile_s=pltpu.SMEM((1, rounds), jnp.int32),
        count_s=pltpu.SMEM((1, 1), jnp.int32),
        lsem=pltpu.SemaphoreType.DMA((11,)),
        ssem=pltpu.SemaphoreType.DMA((6 + n_upper,)),
        frsem=pltpu.SemaphoreType.DMA((rounds,)),
        grsem=pltpu.SemaphoreType.DMA((rounds,)),
        crsem=pltpu.SemaphoreType.DMA((CHUNKS,)),
        rrsem=pltpu.SemaphoreType.DMA((CHUNKS,)),
        xrsem=pltpu.SemaphoreType.DMA((max(n_upper, 1) * CHUNKS,)),
        arsem=pltpu.SemaphoreType.DMA((CHUNKS,)),
        trsem=pltpu.SemaphoreType.DMA((1,)),
    )


def kernel(names, nbits, *refs):
    (features, weight, grad_out, adjacency, stale_feat, stale_grad, blend,
     row_hbm, src_hbm, tile_hbm, count_hbm, out_any, gf_any, gw_any) = refs[:14]
    s = dict(zip(names, refs[14:]))
    send_tile = s["tile_s"]
    tiles, block, width = s["feat"].shape
    rounds = s["fsend"].shape[0]
    entries = s["adj"].shape[0]
    nodes = tiles * block
    cells = tiles + rounds
    half = width // 2
    chunk = half // CHUNKS
    piece = chunk // GROUP
    me = Index(lax.axis_index("dom"), nbits)
    core = bit_of(me.value, 0)
    spot = Index(lax.rem(lax.div(me.value, 2), GROUP), GROUP_BITS)
    upper = upper_stages(nbits)

    def remote(src, dst, send, recv, mask):
        pltpu.make_async_remote_copy(
            src_ref=src, dst_ref=dst, send_sem=send, recv_sem=recv,
            device_id=(me.flip(mask),), device_id_type=MESH).start()

    def settle(ref, sem):
        pltpu.make_async_copy(ref, ref, sem).wait()

    loads = {}
    for i, (src, name) in enumerate((
            (tile_hbm, "tile_s"), (features, "feat"), (row_hbm, "row_s"), (src_hbm, "src_s"),
            (count_hbm, "count_s"), (adjacency, "adj"), (blend, "mixv"), (stale_feat.at[0], "sfeat"),
            (weight, "wgt"), (grad_out, "gout"), (stale_grad, "sgrad"))):
        loads[name] = pltpu.make_async_copy(src, s[name], s["lsem"].at[i])
        loads[name].start()

    round_mask = [1 << (r * nbits // rounds) for r in range(rounds)]
    peers = {1} | {k << 1 for k in range(1, GROUP)} | set(round_mask)
    for lo, nb in upper:
        peers |= {k << lo for k in range(1, 1 << nb)}
    barrier = pltpu.get_barrier_semaphore()
    for m in sorted(peers):
        pl.semaphore_signal(barrier, inc=1, device_id=(me.flip(m),), device_id_type=MESH)

    early = [0] + list(range(3, rounds))
    late = [r for r in range(rounds) if r not in early]
    place = {r: i for i, r in enumerate(early + late)}
    loads["tile_s"].wait()
    loads["feat"].wait()
    for r in late + early[::-1]:
        s["fsend"][r] = s["feat"][send_tile[0, r]]
    pl.semaphore_wait(barrier, len(peers))
    for r in late + early[::-1]:
        remote(s["fsend"].at[r], s["frecv"].at[r], s["ssem"].at[0], s["frsem"].at[r], round_mask[r])

    for name in ("row_s", "src_s", "count_s"):
        loads[name].wait()
    live = s["count_s"][0, 0]
    keys = [jnp.where(e < live, s["row_s"][0, e] * cells + s["src_s"][0, e], -1 - e) for e in range(entries)]
    loads["adj"].wait()
    s["chain"][0] = jnp.zeros((block, block), F32)
    for e in range(entries):
        prev = jnp.int32(0)
        for f in range(e):
            prev = jnp.where(keys[f] == keys[e], f + 1, prev)
        s["chain"][e + 1] = s["chain"][prev] + s["adj"][e].astype(F32)
    for t in range(tiles):
        for c in range(cells):
            last = jnp.int32(0)
            for e in range(entries):
                last = jnp.where(keys[e] == t * cells + c, e + 1, last)
            at = c if c < tiles else tiles + place[c - tiles]
            s["dense"][t * block:(t + 1) * block, at * block:(at + 1) * block] = s["chain"][last].astype(BF16)

    loads["mixv"].wait()
    mix = s["mixv"][...]
    keep = 1.0 - mix
    s["part"][...] = jnp.dot(s["dense"][:, :nodes], s["feat"][...].reshape(nodes, width),
                             preferred_element_type=F32)
    eye = (lax.broadcasted_iota(jnp.int32, (block, block), 0)
           == lax.broadcasted_iota(jnp.int32, (block, block), 1)).astype(F32)
    for t in range(tiles):
        for r in range(rounds):
            hot = jnp.where(send_tile[0, r] == t, 1.0, 0.0).astype(F32)
            s["pick"][t * block:(t + 1) * block, r * block:(r + 1) * block] = (eye * hot).astype(BF16)
    loads["sfeat"].wait()
    loads["wgt"].wait()
    loads["gout"].wait()

    def blend_in(which):
        for r in which:
            pltpu.make_async_copy(s["frecv"].at[r], s["frecv"].at[r], s["frsem"].at[r]).wait()
            at = place[r]
            s["used"][at * block:(at + 1) * block, :] = (
                keep * s["sfeat"][r].astype(F32) + mix * s["frecv"][r].astype(F32)).astype(BF16)

    split = len(early) * block
    blend_in(early)
    s["part"][...] += jnp.dot(s["dense"][:, nodes:nodes + split], s["used"][:split, :],
                              preferred_element_type=F32)
    blend_in(late)
    step = 2 * block
    for t in range(nodes // step):
        rows = slice(t * step, (t + 1) * step)
        agg = (s["part"][rows, :] + jnp.dot(
            s["dense"][rows, nodes + split:], s["used"][split:, :],
            preferred_element_type=F32)).astype(BF16)
        s["aggt"][:, rows] = agg.T
        pre = jnp.dot(agg, s["wgt"][...], preferred_element_type=F32)
        sigma = jax.nn.sigmoid(pre)
        out = pre * sigma
        s["outv"][rows, :] = out.astype(BF16)
        s["dpre"][rows, :] = (s["gout"][rows, :].astype(F32) * sigma * (1.0 + pre * (1.0 - sigma))).astype(BF16)

    def half_product(h):
        return jnp.dot(s["aggt"][pl.ds(pl.multiple_of(h * half, half), half), :], s["dpre"][...],
                       preferred_element_type=F32)

    s["s0send"][...] = half_product(1 - core).astype(BF16)
    for q in range(CHUNKS):
        rows = pl.ds(q * chunk, chunk)
        remote(s["s0send"].at[rows], s["s0recv"].at[rows], s["ssem"].at[1], s["crsem"].at[q], 1)
    s["acc"][...] = half_product(core)
    out_copy = pltpu.make_async_copy(s["outv"], out_any, s["lsem"].at[0])
    out_copy.start()

    def own_rows(q, k=0):
        return pl.ds(pl.multiple_of(q * chunk + spot.flip(k) * piece, piece), piece)

    for q in range(CHUNKS):
        rows = slice(q * chunk, (q + 1) * chunk)
        settle(s["s0recv"].at[pl.ds(q * chunk, chunk)], s["crsem"].at[q])
        total = s["acc"][rows, :] + s["s0recv"][rows, :].astype(F32)
        s["acc"][rows, :] = total
        s["s1send"][rows, :] = total.astype(BF16)
        for k in NEAR_LAST:
            remote(s["s1send"].at[own_rows(q, k)], s["s1recv"].at[q, pl.ds((k - 1) * piece, piece)],
                   s["ssem"].at[2], s["rrsem"].at[q], k << 1)

    s["dagg"][...] = lax.dot_general(s["dpre"][...], s["wgt"][...], (((1,), (1,)), ((), ())),
                                     preferred_element_type=F32).astype(BF16)
    sent = lax.dot_general(s["dense"][:, nodes:], s["dagg"][...], (((0,), (0,)), ((), ())),
                           preferred_element_type=F32).astype(BF16)
    for r in range(rounds):
        s["gsend"][r * block:(r + 1) * block, :] = sent[place[r] * block:(place[r] + 1) * block, :]

    def send_back(r):
        rows = pl.ds(r * block, block)
        remote(s["gsend"].at[rows], s["grecv"].at[rows], s["ssem"].at[5], s["grsem"].at[r], round_mask[r])

    for r in early[:1]:
        send_back(r)
    loads["sgrad"].wait()
    s["back"][...] = lax.dot_general(s["dense"][:, :nodes], s["dagg"][...], (((0,), (0,)), ((), ())),
                                     preferred_element_type=F32) + keep * jnp.dot(
        s["pick"][...], s["sgrad"][...], preferred_element_type=F32)

    totals = []

    def swap(g, q, total):
        lo, nb = upper[g]
        at = lax.rem(lax.div(me.value, 1 << lo), 1 << nb)
        s["xbuf"][g, q, pl.ds(at, 1)] = total.astype(BF16)[None]
        for k in range(1, 1 << nb):
            remote(s["xbuf"].at[g, q, at], s["xbuf"].at[g, q, at], s["ssem"].at[6 + g],
                   s["xrsem"].at[g * CHUNKS + q], k << lo)

    def swapped(g, q):
        size = 1 << upper[g][1]
        settle(s["xbuf"].at[g, q, pl.ds(0, size - 1)], s["xrsem"].at[g * CHUNKS + q])
        total = s["xbuf"][g, q, 0].astype(F32)
        for x in range(1, size):
            total = total + s["xbuf"][g, q, x].astype(F32)
        return total

    def gw_rows(q):
        return pl.ds(pl.multiple_of(core * half + q * chunk + spot.value * piece, piece), piece)

    def spread(q, total):
        s["mine"][q] = total.astype(BF16)
        for k in NEAR_LAST:
            remote(s["mine"].at[q], gw_any.at[gw_rows(q)], s["ssem"].at[3], s["arsem"].at[q], k << 1)
        own = pltpu.make_async_copy(s["mine"].at[q], gw_any.at[gw_rows(q)], s["lsem"].at[1 + q])
        own.start()
        return own

    owns = []
    for q in range(CHUNKS):
        settle(s["s1recv"].at[q], s["rrsem"].at[q])
        total = s["acc"][own_rows(q), :]
        for k in range(1, GROUP):
            total = total + s["s1recv"][q, (k - 1) * piece:k * piece, :].astype(F32)
        if upper:
            swap(0, q, total)
        else:
            owns.append(spread(q, total))
    for r in range(rounds):
        if r not in early[:1]:
            send_back(r)
    for g in range(len(upper)):
        for q in range(CHUNKS):
            total = swapped(g, q)
            if g + 1 < len(upper):
                swap(g + 1, q, total)
            else:
                owns.append(spread(q, total))

    for r in range(rounds):
        rows = pl.ds(r * block, block)
        settle(s["grecv"].at[rows], s["grsem"].at[r])
    s["gfeat"][...] = (s["back"][...] + mix * jnp.dot(
        s["pick"][...], s["grecv"][...], preferred_element_type=F32)).astype(BF16)
    gf_copy = pltpu.make_async_copy(s["gfeat"], gf_any, s["lsem"].at[1 + CHUNKS])
    gf_copy.start()

    for q in range(CHUNKS):
        settle(s["s1recv"].at[q], s["arsem"].at[q])
        owns[q].wait()
        rows = pl.ds(pl.multiple_of(core * half + q * chunk, chunk), chunk)
        remote(gw_any.at[rows], gw_any.at[rows], s["ssem"].at[4], s["trsem"].at[0], 1)

    settle(s["fsend"], s["ssem"].at[0])
    settle(s["s0send"], s["ssem"].at[1])
    settle(s["s1recv"], s["ssem"].at[2])
    settle(s["s1recv"], s["ssem"].at[3])
    settle(s["gsend"], s["ssem"].at[5])
    for g, (lo, nb) in enumerate(upper):
        settle(s["xbuf"].at[g, :, pl.ds(0, (1 << nb) - 1)], s["ssem"].at[6 + g])
    out_copy.wait()
    gf_copy.wait()
    settle(s["s0recv"], s["trsem"].at[0])
    settle(s["s0recv"], s["ssem"].at[4])


def finish(*refs):
    ins, outs, sem = refs[:3], refs[3:6], refs[6]
    copies = [pltpu.make_async_copy(a, b, sem.at[i]) for i, (a, b) in enumerate(zip(ins, outs))]
    for c in copies:
        c.start()
    for c in copies:
        c.wait()


def body(nbits, features, weight, grad_out, adjacency, tile_row, tile_src, tile_count,
         send_tile, stale_feat, stale_grad, blend):
    nodes, width = features.shape
    entries, block = adjacency.shape[:2]
    rounds = send_tile.shape[1]
    tiles = nodes // block
    scratch = names_and_shapes(tiles, block, width, entries, rounds, len(upper_stages(nbits)))
    hbm = pl.BlockSpec(memory_space=pltpu.HBM)
    free = pl.BlockSpec(memory_space=pl.ANY)
    results = (jax.ShapeDtypeStruct((nodes, width), BF16),
               jax.ShapeDtypeStruct((nodes, width), BF16),
               jax.ShapeDtypeStruct((width, width), BF16))
    found = pl.pallas_call(
        functools.partial(kernel, tuple(scratch), nbits),
        name="layer",
        out_shape=results,
        in_specs=[hbm] * 10 + [free],
        out_specs=(free,) * 3,
        scratch_shapes=list(scratch.values()),
        compiler_params=pltpu.CompilerParams(collective_id=0, has_side_effects=True,
                                             vmem_limit_bytes=48 * 1024 * 1024),
    )(*(pltpu.with_memory_space_constraint(x, pltpu.HBM) for x in (
        features.reshape(tiles, block, width), weight, grad_out, adjacency, stale_feat,
        stale_grad.reshape(rounds * block, width), blend.reshape(1, width),
        tile_row, tile_src, send_tile)), tile_count.reshape(1, 1))
    return tuple(pl.pallas_call(
        finish,
        name="finish",
        out_shape=results,
        in_specs=[free] * 3,
        out_specs=(hbm,) * 3,
        scratch_shapes=[pltpu.SemaphoreType.DMA((3,))],
        compiler_params=pltpu.CompilerParams(vmem_limit_bytes=16 * 1024 * 1024),
    )(*found))


def solution(mesh):
    nbits = mesh.shape["dom"].bit_length() - 1
    placed = (
        P("dom", None), P(), P("dom", None), P("dom", None, None), P("dom", None), P("dom", None),
        P("dom"), P("dom", None), P("dom", None, None, None), P("dom", None, None, None), P(),
    )
    return jax.shard_map(
        functools.partial(body, nbits),
        mesh=mesh,
        in_specs=placed,
        out_specs=(P("dom", None), P("dom", None), P()),
        check_vma=False,
    )
```

time: 32.3 us -> 29.3 us (0.907)
  Pallas kernels: 30.8 us -> 27.9 us
    pallas_call x1, Pallas kernels: 29.7 us -> 26.7 us  [body(): pl.pallas_call(functools.partial(kernel, tuple(scratch), nbits), name='la...]
where the time goes in v1:
time: 29.3 us; the launch traced here: 29.2 us
  Pallas kernels  27.9 us (95%)
  between operations  1.29 us (4%)
    pallas_call x1, Pallas kernels, body(): pl.pallas_call(functools.partial(kernel, tuple(scratch), nbits), name='la...  26.7 us
    pallas_call x1, Pallas kernels, body(): pl.pallas_call(finish, name='finish', out_shape=results, in_specs=[free]...  1.17 us

profile of v1, /device:TPU:0, one launch (start us, length us, event | category | flops | bytes accessed | tf_op | source)
XLA Modules:
  0.0 29.2 jit_solution(4956663225098935182)
XLA Ops:
  1.3 26.7 %layer.1 = (bf16[512,512]{1,0:T(8,128)(2,1)S(1)}, bf16[512,512]{1,0:T(8,128)(2,1)S(1)}, bf16[512,512]{1,0:T(8,128)(2,1)S(1)}) custom-call(bf16[4,128,512]{2,1,0:T(8,128)(2,1)} %bitcast.5, bf16[512,512]{1,0:T(8,128)(2,1)} %refs_1_.1, bf16[512,512]{1,0:T(8,128)(2,1)} %refs_2_.1, bf16[24,128,128]{2,1,0:T(8,128)(2,1)} %refs_3_.1, ...), custom_call_target="tpu_custom_call" | custom-call | tf_op jit(solution)/shard_map/layer/pallas_call | solution.py:348
  28.0 1.2 %finish.1 = (bf16[512,512]{1,0:T(8,128)(2,1)}, bf16[512,512]{1,0:T(8,128)(2,1)}, bf16[512,512]{1,0:T(8,128)(2,1)}) custom-call(bf16[512,512]{1,0:T(8,128)(2,1)S(1)} %get-tuple-element.6.refs_0_, bf16[512,512]{1,0:T(8,128)(2,1)S(1)} %get-tuple-element.7.refs_1_, bf16[512,512]{1,0:T(8,128)(2,1)S(1)} %get-tuple-element.8.refs_2_), custom_call_target="tpu_custom_call" | custom-call | tf_op jit(solution)/shard_map/finish/pallas_call | solution.py:361

commit v2 on v1

--- a/solution.py
+++ b/solution.py
@@ -59,15 +59,15 @@
         chain=v((entries + 1, block, block), F32),
         dense=v((nodes, (tiles + rounds) * block), BF16),
         pick=v((nodes, rounds * block), BF16),
+        edge=v((rounds * block, nodes), BF16),
+        wgtt=v((width, width), BF16),
         part=v((nodes, width), F32),
         aggt=v((width, nodes), BF16),
-        outv=v((nodes, width), BF16),
         dpre=v((nodes, width), BF16),
         dagg=v((nodes, width), BF16),
         back=v((nodes, width), F32),
         gsend=v((rounds * block, width), BF16),
         grecv=v((rounds * block, width), BF16),
-        gfeat=v((nodes, width), BF16),
         s0send=v((half, width), BF16),
         s0recv=v((half, width), BF16),
         acc=v((half, width), F32),
@@ -118,6 +118,14 @@
     def settle(ref, sem):
         pltpu.make_async_copy(ref, ref, sem).wait()
 
+    round_mask = [1 << (r * nbits // rounds) for r in range(rounds)]
+    peers = {1} | {k << 1 for k in range(1, GROUP)} | set(round_mask)
+    for lo, nb in upper:
+        peers |= {k << lo for k in range(1, 1 << nb)}
+    barrier = pltpu.get_barrier_semaphore()
+    for m in sorted(peers):
+        pl.semaphore_signal(barrier, inc=1, device_id=(me.flip(m),), device_id_type=MESH)
+
     loads = {}
     for i, (src, name) in enumerate((
             (tile_hbm, "tile_s"), (features, "feat"), (row_hbm, "row_s"), (src_hbm, "src_s"),
@@ -125,14 +133,6 @@
             (weight, "wgt"), (grad_out, "gout"), (stale_grad, "sgrad"))):
         loads[name] = pltpu.make_async_copy(src, s[name], s["lsem"].at[i])
         loads[name].start()
-
-    round_mask = [1 << (r * nbits // rounds) for r in range(rounds)]
-    peers = {1} | {k << 1 for k in range(1, GROUP)} | set(round_mask)
-    for lo, nb in upper:
-        peers |= {k << lo for k in range(1, 1 << nb)}
-    barrier = pltpu.get_barrier_semaphore()
-    for m in sorted(peers):
-        pl.semaphore_signal(barrier, inc=1, device_id=(me.flip(m),), device_id_type=MESH)
 
     early = [0] + list(range(3, rounds))
     late = [r for r in range(rounds) if r not in early]
@@ -162,7 +162,10 @@
             for e in range(entries):
                 last = jnp.where(keys[e] == t * cells + c, e + 1, last)
             at = c if c < tiles else tiles + place[c - tiles]
-            s["dense"][t * block:(t + 1) * block, at * block:(at + 1) * block] = s["chain"][last].astype(BF16)
+            cell = s["chain"][last].astype(BF16)
+            s["dense"][t * block:(t + 1) * block, at * block:(at + 1) * block] = cell
+            if c >= tiles:
+                s["edge"][(c - tiles) * block:(c - tiles + 1) * block, t * block:(t + 1) * block] = cell.T
 
     loads["mixv"].wait()
     mix = s["mixv"][...]
@@ -177,6 +180,7 @@
             s["pick"][t * block:(t + 1) * block, r * block:(r + 1) * block] = (eye * hot).astype(BF16)
     loads["sfeat"].wait()
     loads["wgt"].wait()
+    s["wgtt"][...] = s["wgt"][...].T
     loads["gout"].wait()
 
     def blend_in(which):
@@ -201,20 +205,33 @@
         pre = jnp.dot(agg, s["wgt"][...], preferred_element_type=F32)
         sigma = jax.nn.sigmoid(pre)
         out = pre * sigma
-        s["outv"][rows, :] = out.astype(BF16)
+        out_any[rows, :] = out.astype(BF16)
         s["dpre"][rows, :] = (s["gout"][rows, :].astype(F32) * sigma * (1.0 + pre * (1.0 - sigma))).astype(BF16)
 
-    def half_product(h):
-        return jnp.dot(s["aggt"][pl.ds(pl.multiple_of(h * half, half), half), :], s["dpre"][...],
+    def chunk_product(h, q):
+        return jnp.dot(s["aggt"][pl.ds(pl.multiple_of(h * half + q * chunk, chunk), chunk), :], s["dpre"][...],
                        preferred_element_type=F32)
 
-    s["s0send"][...] = half_product(1 - core).astype(BF16)
     for q in range(CHUNKS):
         rows = pl.ds(q * chunk, chunk)
+        s["s0send"][q * chunk:(q + 1) * chunk, :] = chunk_product(1 - core, q).astype(BF16)
         remote(s["s0send"].at[rows], s["s0recv"].at[rows], s["ssem"].at[1], s["crsem"].at[q], 1)
-    s["acc"][...] = half_product(core)
-    out_copy = pltpu.make_async_copy(s["outv"], out_any, s["lsem"].at[0])
-    out_copy.start()
+    for q in range(CHUNKS):
+        s["acc"][q * chunk:(q + 1) * chunk, :] = chunk_product(core, q)
+
+    def send_back(r):
+        rows = pl.ds(r * block, block)
+        remote(s["gsend"].at[rows], s["grecv"].at[rows], s["ssem"].at[5], s["grsem"].at[r], round_mask[r])
+
+    def make_back():
+        s["dagg"][...] = jnp.dot(s["dpre"][...], s["wgtt"][...], preferred_element_type=F32).astype(BF16)
+        s["gsend"][...] = jnp.dot(s["edge"][...], s["dagg"][...], preferred_element_type=F32).astype(BF16)
+
+    @pl.when(core == 1)
+    def _():
+        make_back()
+        for r in late + early[::-1]:
+            send_back(r)
 
     def own_rows(q, k=0):
         return pl.ds(pl.multiple_of(q * chunk + spot.flip(k) * piece, piece), piece)
@@ -229,19 +246,12 @@
             remote(s["s1send"].at[own_rows(q, k)], s["s1recv"].at[q, pl.ds((k - 1) * piece, piece)],
                    s["ssem"].at[2], s["rrsem"].at[q], k << 1)
 
-    s["dagg"][...] = lax.dot_general(s["dpre"][...], s["wgt"][...], (((1,), (1,)), ((), ())),
-                                     preferred_element_type=F32).astype(BF16)
-    sent = lax.dot_general(s["dense"][:, nodes:], s["dagg"][...], (((0,), (0,)), ((), ())),
-                           preferred_element_type=F32).astype(BF16)
-    for r in range(rounds):
-        s["gsend"][r * block:(r + 1) * block, :] = sent[place[r] * block:(place[r] + 1) * block, :]
-
-    def send_back(r):
-        rows = pl.ds(r * block, block)
-        remote(s["gsend"].at[rows], s["grecv"].at[rows], s["ssem"].at[5], s["grsem"].at[r], round_mask[r])
-
-    for r in early[:1]:
-        send_back(r)
+    @pl.when(core == 0)
+    def _():
+        make_back()
+        for r in early[:1]:
+            send_back(r)
+
     loads["sgrad"].wait()
     s["back"][...] = lax.dot_general(s["dense"][:, :nodes], s["dagg"][...], (((0,), (0,)), ((), ())),
                                      preferred_element_type=F32) + keep * jnp.dot(
@@ -286,9 +296,11 @@
             swap(0, q, total)
         else:
             owns.append(spread(q, total))
-    for r in range(rounds):
-        if r not in early[:1]:
+    @pl.when(core == 0)
+    def _():
+        for r in late + early[:0:-1]:
             send_back(r)
+
     for g in range(len(upper)):
         for q in range(CHUNKS):
             total = swapped(g, q)
@@ -300,10 +312,8 @@
     for r in range(rounds):
         rows = pl.ds(r * block, block)
         settle(s["grecv"].at[rows], s["grsem"].at[r])
-    s["gfeat"][...] = (s["back"][...] + mix * jnp.dot(
+    gf_any[...] = (s["back"][...] + mix * jnp.dot(
         s["pick"][...], s["grecv"][...], preferred_element_type=F32)).astype(BF16)
-    gf_copy = pltpu.make_async_copy(s["gfeat"], gf_any, s["lsem"].at[1 + CHUNKS])
-    gf_copy.start()
 
     for q in range(CHUNKS):
         settle(s["s1recv"].at[q], s["arsem"].at[q])
@@ -318,8 +328,6 @@
     settle(s["gsend"], s["ssem"].at[5])
     for g, (lo, nb) in enumerate(upper):
         settle(s["xbuf"].at[g, :, pl.ds(0, (1 << nb) - 1)], s["ssem"].at[6 + g])
-    out_copy.wait()
-    gf_copy.wait()
     settle(s["s0recv"], s["trsem"].at[0])
     settle(s["s0recv"], s["ssem"].at[4])
 
@@ -350,7 +358,7 @@
         name="layer",
         out_shape=results,
         in_specs=[hbm] * 10 + [free],
-        out_specs=(free,) * 3,
+        out_specs=(pl.BlockSpec(memory_space=pltpu.VMEM),) * 2 + (free,),
         scratch_shapes=list(scratch.values()),
         compiler_params=pltpu.CompilerParams(collective_id=0, has_side_effects=True,
                                              vmem_limit_bytes=48 * 1024 * 1024),

time: 29.3 us -> 28.7 us (0.980)
  Pallas kernels: 27.9 us -> 27.3 us
    pallas_call x1, Pallas kernels: 26.7 us -> 26.1 us  [body(): pl.pallas_call(functools.partial(kernel, tuple(scratch), nbits), name='la...]
where the time goes in v2:
time: 28.7 us; the launch traced here: 28.6 us
  Pallas kernels  27.3 us (95%)
  between operations  1.29 us (4%)
    pallas_call x1, Pallas kernels, body(): pl.pallas_call(functools.partial(kernel, tuple(scratch), nbits), name='la...  26.1 us
    pallas_call x1, Pallas kernels, body(): pl.pallas_call(finish, name='finish', out_shape=results, in_specs=[free]...  1.17 us

profile of v2, /device:TPU:0, one launch (start us, length us, event | category | flops | bytes accessed | tf_op | source)
XLA Modules:
  0.0 28.6 jit_solution(12633907874418137936)
XLA Ops:
  1.3 26.1 %layer.1 = (bf16[512,512]{1,0:T(8,128)(2,1)S(1)}, bf16[512,512]{1,0:T(8,128)(2,1)S(1)}, bf16[512,512]{1,0:T(8,128)(2,1)S(1)}) custom-call(bf16[4,128,512]{2,1,0:T(8,128)(2,1)} %bitcast.5, bf16[512,512]{1,0:T(8,128)(2,1)} %refs_1_.1, bf16[512,512]{1,0:T(8,128)(2,1)} %refs_2_.1, bf16[24,128,128]{2,1,0:T(8,128)(2,1)} %refs_3_.1, ...), custom_call_target="tpu_custom_call" | custom-call | tf_op jit(solution)/shard_map/layer/pallas_call | solution.py:356
  27.4 1.2 %finish.1 = (bf16[512,512]{1,0:T(8,128)(2,1)}, bf16[512,512]{1,0:T(8,128)(2,1)}, bf16[512,512]{1,0:T(8,128)(2,1)}) custom-call(bf16[512,512]{1,0:T(8,128)(2,1)S(1)} %get-tuple-element.6.refs_0_, bf16[512,512]{1,0:T(8,128)(2,1)S(1)} %get-tuple-element.7.refs_1_, bf16[512,512]{1,0:T(8,128)(2,1)S(1)} %get-tuple-element.8.refs_2_), custom_call_target="tpu_custom_call" | custom-call | tf_op jit(solution)/shard_map/finish/pallas_call | solution.py:369

commit v3 on v2

--- a/solution.py
+++ b/solution.py
@@ -83,11 +83,11 @@
         lsem=pltpu.SemaphoreType.DMA((11,)),
         ssem=pltpu.SemaphoreType.DMA((6 + n_upper,)),
         frsem=pltpu.SemaphoreType.DMA((rounds,)),
-        grsem=pltpu.SemaphoreType.DMA((rounds,)),
+        grsem=pltpu.SemaphoreType.DMA((1,)),
         crsem=pltpu.SemaphoreType.DMA((CHUNKS,)),
         rrsem=pltpu.SemaphoreType.DMA((CHUNKS,)),
         xrsem=pltpu.SemaphoreType.DMA((max(n_upper, 1) * CHUNKS,)),
-        arsem=pltpu.SemaphoreType.DMA((CHUNKS,)),
+        arsem=pltpu.SemaphoreType.DMA((CHUNKS - 1 + GROUP - 1,)),
         trsem=pltpu.SemaphoreType.DMA((1,)),
     )
 
@@ -221,7 +221,7 @@
 
     def send_back(r):
         rows = pl.ds(r * block, block)
-        remote(s["gsend"].at[rows], s["grecv"].at[rows], s["ssem"].at[5], s["grsem"].at[r], round_mask[r])
+        remote(s["gsend"].at[rows], s["grecv"].at[rows], s["ssem"].at[5], s["grsem"].at[0], round_mask[r])
 
     def make_back():
         s["dagg"][...] = jnp.dot(s["dpre"][...], s["wgtt"][...], preferred_element_type=F32).astype(BF16)
@@ -281,7 +281,8 @@
     def spread(q, total):
         s["mine"][q] = total.astype(BF16)
         for k in NEAR_LAST:
-            remote(s["mine"].at[q], gw_any.at[gw_rows(q)], s["ssem"].at[3], s["arsem"].at[q], k << 1)
+            remote(s["mine"].at[q], gw_any.at[gw_rows(q)], s["ssem"].at[3],
+                   s["arsem"].at[q if q < CHUNKS - 1 else q + k - 1], k << 1)
         own = pltpu.make_async_copy(s["mine"].at[q], gw_any.at[gw_rows(q)], s["lsem"].at[1 + q])
         own.start()
         return own
@@ -309,16 +310,22 @@
             else:
                 owns.append(spread(q, total))
 
-    for r in range(rounds):
-        rows = pl.ds(r * block, block)
-        settle(s["grecv"].at[rows], s["grsem"].at[r])
+    settle(s["grecv"], s["grsem"].at[0])
     gf_any[...] = (s["back"][...] + mix * jnp.dot(
         s["pick"][...], s["grecv"][...], preferred_element_type=F32)).astype(BF16)
 
-    for q in range(CHUNKS):
+    for q in range(CHUNKS - 1):
         settle(s["s1recv"].at[q], s["arsem"].at[q])
         owns[q].wait()
         rows = pl.ds(pl.multiple_of(core * half + q * chunk, chunk), chunk)
+        remote(gw_any.at[rows], gw_any.at[rows], s["ssem"].at[4], s["trsem"].at[0], 1)
+    q = CHUNKS - 1
+    for k in (0,) + NEAR_LAST[::-1]:
+        rows = pl.ds(pl.multiple_of(core * half + q * chunk + spot.flip(k) * piece, piece), piece)
+        if k:
+            settle(gw_any.at[rows], s["arsem"].at[q + k - 1])
+        else:
+            owns[q].wait()
         remote(gw_any.at[rows], gw_any.at[rows], s["ssem"].at[4], s["trsem"].at[0], 1)
 
     settle(s["fsend"], s["ssem"].at[0])

time: 28.7 us -> 28.6 us (level)
  no operation moved by 1% of the time
where the time goes in v3:
time: 28.6 us; the launch traced here: 28.5 us
  Pallas kernels  27.2 us (95%)
  between operations  1.29 us (5%)
    pallas_call x1, Pallas kernels, body(): pl.pallas_call(functools.partial(kernel, tuple(scratch), nbits), name='la...  26 us
    pallas_call x1, Pallas kernels, body(): pl.pallas_call(finish, name='finish', out_shape=results, in_specs=[free]...  1.17 us

profile of v3, /device:TPU:0, one launch (start us, length us, event | category | flops | bytes accessed | tf_op | source)
XLA Modules:
  0.0 28.5 jit_solution(13047308062408057431)
XLA Ops:
  1.3 26.0 %layer.1 = (bf16[512,512]{1,0:T(8,128)(2,1)S(1)}, bf16[512,512]{1,0:T(8,128)(2,1)S(1)}, bf16[512,512]{1,0:T(8,128)(2,1)S(1)}) custom-call(bf16[4,128,512]{2,1,0:T(8,128)(2,1)} %bitcast.5, bf16[512,512]{1,0:T(8,128)(2,1)} %refs_1_.1, bf16[512,512]{1,0:T(8,128)(2,1)} %refs_2_.1, bf16[24,128,128]{2,1,0:T(8,128)(2,1)} %refs_3_.1, ...), custom_call_target="tpu_custom_call" | custom-call | tf_op jit(solution)/shard_map/layer/pallas_call | solution.py:363
  27.3 1.2 %finish.1 = (bf16[512,512]{1,0:T(8,128)(2,1)}, bf16[512,512]{1,0:T(8,128)(2,1)}, bf16[512,512]{1,0:T(8,128)(2,1)}) custom-call(bf16[512,512]{1,0:T(8,128)(2,1)S(1)} %get-tuple-element.6.refs_0_, bf16[512,512]{1,0:T(8,128)(2,1)S(1)} %get-tuple-element.7.refs_1_, bf16[512,512]{1,0:T(8,128)(2,1)S(1)} %get-tuple-element.8.refs_2_), custom_call_target="tpu_custom_call" | custom-call | tf_op jit(solution)/shard_map/finish/pallas_call | solution.py:376

commit v4 on v3

--- a/solution.py
+++ b/solution.py
@@ -295,11 +295,16 @@
             total = total + s["s1recv"][q, (k - 1) * piece:k * piece, :].astype(F32)
         if upper:
             swap(0, q, total)
+            if q == 0:
+                @pl.when(core == 0)
+                def _():
+                    for r in late:
+                        send_back(r)
         else:
             owns.append(spread(q, total))
     @pl.when(core == 0)
     def _():
-        for r in late + early[:0:-1]:
+        for r in early[:0:-1]:
             send_back(r)
 
     for g in range(len(upper)):

time: 28.6 us -> 28.6 us (level)
  no operation moved by 1% of the time
where the time goes in v4:
time: 28.6 us; the launch traced here: 28.5 us
  Pallas kernels  27.2 us (95%)
  between operations  1.29 us (5%)
    pallas_call x1, Pallas kernels, body(): pl.pallas_call(functools.partial(kernel, tuple(scratch), nbits), name='la...  26 us
    pallas_call x1, Pallas kernels, body(): pl.pallas_call(finish, name='finish', out_shape=results, in_specs=[free]...  1.17 us

profile of v4, /device:TPU:0, one launch (start us, length us, event | category | flops | bytes accessed | tf_op | source)
XLA Modules:
  0.0 28.5 jit_solution(8706954800802058363)
XLA Ops:
  1.3 26.0 %layer.1 = (bf16[512,512]{1,0:T(8,128)(2,1)S(1)}, bf16[512,512]{1,0:T(8,128)(2,1)S(1)}, bf16[512,512]{1,0:T(8,128)(2,1)S(1)}) custom-call(bf16[4,128,512]{2,1,0:T(8,128)(2,1)} %bitcast.5, bf16[512,512]{1,0:T(8,128)(2,1)} %refs_1_.1, bf16[512,512]{1,0:T(8,128)(2,1)} %refs_2_.1, bf16[24,128,128]{2,1,0:T(8,128)(2,1)} %refs_3_.1, ...), custom_call_target="tpu_custom_call" | custom-call | tf_op jit(solution)/shard_map/layer/pallas_call | solution.py:368
  27.3 1.2 %finish.1 = (bf16[512,512]{1,0:T(8,128)(2,1)}, bf16[512,512]{1,0:T(8,128)(2,1)}, bf16[512,512]{1,0:T(8,128)(2,1)}) custom-call(bf16[512,512]{1,0:T(8,128)(2,1)S(1)} %get-tuple-element.6.refs_0_, bf16[512,512]{1,0:T(8,128)(2,1)S(1)} %get-tuple-element.7.refs_1_, bf16[512,512]{1,0:T(8,128)(2,1)S(1)} %get-tuple-element.8.refs_2_), custom_call_target="tpu_custom_call" | custom-call | tf_op jit(solution)/shard_map/finish/pallas_call | solution.py:381
